TPU v7x, 512 devices: a whole 4x8x8 slice. The times are simulated.
512 devices in a mesh: leaf: 128 (over z, y, core), sep: 4 (over x).
Axes of the slice: x: 4, y: 8, z: 8, core: 2. Of those that a mesh axis runs over, the one named last changes fastest.
Arguments:
- leaf_source: float32 [128, 640, 256], P('leaf', 'sep'), may hold values from -6 to 6
- leaf_inverse: float32 [128, 640, 640], P('leaf', 'sep'), as said below
- leaf_update: float32 [128, 896, 640], P('leaf', None, 'sep'), as said below
- row_lists: int32 [128, 896], P('leaf'), may hold values from 0 to 255
- row_counts: int32 [128, 7], P('leaf'), may hold values from 1 to 128, as said below
- separator_source: float32 [128, 256, 256], P('leaf', 'sep'), may hold values from -6 to 6
- separator_inverse: float32 [128, 256, 256], P('leaf'), as said below
- separator_coupling: float32 [128, 256, 256], P('leaf'), may hold values from -0.1875 to 0.1875
Outputs:
- leaf_solution: float32 [128, 640, 256], P('leaf', 'sep')
- separator_solution: float32 [128, 256, 256], P('leaf', 'sep')
Inputs may be any that keep to these rules, and one draw needn't show every extreme that they name: `leaf_inverse`: each leaf's block is lower triangular, zero above the diagonal, with diagonal entries between 0.6 and 1.4. `separator_inverse`: each block is lower triangular, zero above the diagonal, with diagonal entries between 0.6 and 1.4. `leaf_update`: row r of a leaf's block belongs to the leaf's ancestor of level 1 + r // 128. `row_lists`: entry r names a row of the leaf's ancestor of level 1 + r // 128. `row_counts`: at every level some leaf has 128 live rows.
All inputs are finite; a program needn't handle non-finite values.
Results may differ from a plain program's by a relative error of at most 0.00011.
Values sent between devices are 32-bit elements; how exact they have to be, the bound alone decides.
A program may use at most 64 MiB of HBM per device.

v0:
```python
import jax
import jax.numpy as jnp
from jax import lax
from jax.sharding import PartitionSpec as P

highest = lax.Precision.HIGHEST


def passed_along(x, axis, by):
    peers = lax.axis_size(axis)
    pairs = [(i, i + by) for i in range(peers) if 0 <= i + by < peers]
    return lax.ppermute(x, axis, pairs)


def product(matrix, operand):
    return jnp.dot(matrix, operand, precision=highest, preferred_element_type=jnp.float32)


def product_first(matrix, operand):
    return lax.dot_general(
        matrix,
        operand,
        (((0,), (0,)), ((), ())),
        precision=highest,
        preferred_element_type=jnp.float32,
    )


def tree_pass(payload, offset):
    return passed_along(payload, "leaf", offset)


def sep_rows(payload):
    return lax.all_gather(payload, "sep", axis=0, tiled=True)


def per_device(
    leaf_source,
    leaf_inverse,
    leaf_update,
    row_lists,
    row_counts,
    separator_source,
    separator_inverse,
    separator_coupling,
):
    depth = row_counts.shape[1]
    leaf_index = lax.axis_index("leaf")
    sep_index = lax.axis_index("sep")
    source = leaf_source[0]
    inverse = leaf_inverse[0]
    update = leaf_update[0]
    quarter = separator_source.shape[1]
    full_rows = separator_inverse.shape[1]
    columns = source.shape[1]
    capacity = row_lists.shape[1] // depth
    first_row = sep_index * quarter
    inverse_block = inverse
    leaf_y = product(inverse_block, lax.all_gather(source, "sep", axis=0, tiled=True))
    slot_index = jnp.arange(depth * capacity) % capacity
    limits = jnp.repeat(row_counts[0], capacity)
    live_rows = (slot_index < limits)[:, None]
    update_terms = jnp.where(live_rows, product(update, leaf_y), 0.0)
    targets = row_lists[0].reshape(depth, capacity)
    picker = (jnp.arange(full_rows)[None, :, None] == targets[:, None, :]).astype(jnp.float32)
    densified = jnp.einsum(
        "kwp,kpn->wkn",
        picker,
        update_terms.reshape(depth, capacity, columns),
        precision=highest,
        preferred_element_type=jnp.float32,
    )
    carried = lax.psum_scatter(densified, "sep", scatter_dimension=0, tiled=True)
    own_source = separator_source[0]
    solver_block = separator_inverse[0]
    coupling = separator_coupling[0]
    coupling_rows = lax.dynamic_slice_in_dim(coupling, first_row, quarter, 0)
    solved_down = jnp.zeros((full_rows, columns), jnp.float32)
    for height in range(1, depth + 1):
        upper_slots = carried[:, height - 1 :]
        stride = 2 ** max(height - 2, 0)
        from_left = tree_pass(upper_slots, stride)
        if height == 1:
            from_right = upper_slots
        else:
            from_right = tree_pass(upper_slots, -stride)
        is_owner = leaf_index % 2**height == 2 ** (height - 1)
        carried = carried.at[:, height - 1 :].set(
            jnp.where(is_owner, from_left + from_right, upper_slots)
        )
        residual_full = sep_rows(own_source - carried[:, height - 1])
        solved = product(solver_block, residual_full)
        solved_down = jnp.where(is_owner, solved, solved_down)
        if height < depth:
            carried = carried.at[:, height].add(
                jnp.where(is_owner, product(coupling_rows, solved), 0.0)
            )
    stacked = jnp.zeros(carried.shape, jnp.float32)
    solution_full = jnp.zeros((full_rows, columns), jnp.float32)
    for height in range(depth, 0, -1):
        is_owner = leaf_index % 2**height == 2 ** (height - 1)
        target = solved_down
        if height < depth:
            stride = 2 ** (height - 1)
            upper_slots = stacked[:, height:]
            from_below = tree_pass(upper_slots, stride)
            from_above = tree_pass(upper_slots, -stride)
            right_child = leaf_index // 2**height % 2 == 1
            received = jnp.where(right_child, from_below, from_above)
            stacked = stacked.at[:, height:].set(jnp.where(is_owner, received, upper_slots))
            parent_full = sep_rows(received[:, 0])
            target = solved_down - product_first(coupling, parent_full)
        solution = product_first(solver_block, target)
        solution_full = jnp.where(is_owner, solution, solution_full)
        own_rows = lax.dynamic_slice_in_dim(solution, first_row, quarter, 0)
        stacked = stacked.at[:, height - 1].set(
            jnp.where(is_owner, own_rows, stacked[:, height - 1])
        )
    from_next = tree_pass(stacked, -1)
    ancestors = jnp.where(leaf_index % 2 == 1, stacked, from_next)
    ancestors_full = sep_rows(ancestors)
    picked = jnp.einsum(
        "kwp,wkn->kpn",
        picker,
        ancestors_full,
        precision=highest,
        preferred_element_type=jnp.float32,
    )
    picked = jnp.where(live_rows, picked.reshape(depth * capacity, columns), 0.0)
    leaf_w = leaf_y - product_first(update, picked)
    inverse_block = inverse
    leaf_x = lax.psum_scatter(
        product_first(inverse_block, leaf_w), "sep", scatter_dimension=0, tiled=True
    )
    separator_rows = lax.dynamic_slice_in_dim(solution_full, first_row, quarter, 0)
    return (leaf_x[None], separator_rows[None])


def solution(mesh):
    placed = (
        P("leaf", "sep", None),
        P("leaf", "sep", None),
        P("leaf", None, "sep"),
        P("leaf", None),
        P("leaf", None),
        P("leaf", "sep", None),
        P("leaf", None, None),
        P("leaf", None, None),
    )
    return jax.shard_map(
        per_device,
        mesh=mesh,
        in_specs=placed,
        out_specs=(P("leaf", "sep", None), P("leaf", "sep", None)),
        check_vma=False,
    )
```

profile of v0, /device:TPU:8, one launch (start us, length us, event | category | flops | bytes accessed | tf_op | source)
XLA Modules:
  0.0 518.3 jit_solution(3606953752508697259)
XLA Ops:
  7.2 13.7 %all-gather = f32[1,640,256]{2,1,0:T(8,128)S(1)} all-gather(f32[1,160,256]{2,1,0:T(8,128)} %param.62), channel_id=2, replica_groups=mesh['leaf'=128,'sep'=4] {'sep'}, dimensions={1}, use_global_device_ids=true | all-gather | bytes 819200 | tf_op jit(solution)/shard_map/all_gather | solution.py:59
  21.7 1.6 fusion.8
  25.8 2.0 copy.66
  27.9 39.7 %reduce-scatter.5.cloned.1.call-done = f32[64,7,256]{2,1,0:T(8,128)} async-done(((f32[256,7,256]{2,1,0:T(8,128)}), f32[64,7,256]{2,1,0:T(8,128)}) %reduce-scatter.5.cloned.1.call-update) | async-done | bytes 458768 | tf_op jit(solution)/shard_map/reduce_scatter | solution.py:73
  68.8 1.9 collective-permute-start
  70.7 7.9 %collective-permute-done = f32[64,7,256]{2,0,1:T(8,128)S(1)} collective-permute-done((f32[64,7,256]{2,0,1:T(8,128)S(1)}, f32[64,7,256]{2,0,1:T(8,128)S(1)}, u32[]{:S(2)}, u32[]{:S(2)}) %collective-permute-start) | collective-permute-done | bytes 458784 | tf_op jit(solution)/shard_map/ppermute | solution.py:12
  79.8 12.4 %all_gather.46 = f32[256,256]{1,0:T(8,128)S(1)} all-gather(f32[64,256]{1,0:T(8,128)S(1)} %fusion.94), channel_id=1, replica_groups=mesh['leaf'=128,'sep'=4] {'sep'}, dimensions={0}, use_global_device_ids=true | all-gather | bytes 327680 | tf_op jit(solution)/shard_map/all_gather | solution.py:34
  93.2 1.9 collective-permute-start.1
  95.2 3.6 collective-permute-start.2
  98.8 3.5 collective-permute-done.1
  102.3 1.8 collective-permute-done.2
  104.2 12.5 %all_gather.47 = f32[256,256]{1,0:T(8,128)S(1)} all-gather(f32[64,256]{1,0:T(8,128)S(1)} %fusion.92), channel_id=1, replica_groups=mesh['leaf'=128,'sep'=4] {'sep'}, dimensions={0}, use_global_device_ids=true | all-gather | bytes 327680 | tf_op jit(solution)/shard_map/all_gather | solution.py:34
  117.8 3.4 collective-permute-start.3
  121.2 2.5 collective-permute-start.4
  123.7 4.8 collective-permute-done.3
  128.5 4.6 collective-permute-done.4
  133.2 12.3 %all_gather.48 = f32[256,256]{1,0:T(8,128)S(1)} all-gather(f32[64,256]{1,0:T(8,128)S(1)} %fusion.90), channel_id=1, replica_groups=mesh['leaf'=128,'sep'=4] {'sep'}, dimensions={0}, use_global_device_ids=true | all-gather | bytes 327680 | tf_op jit(solution)/shard_map/all_gather | solution.py:34
  146.5 6.2 %collective-permute-start.5 = (f32[64,4,256]{2,0,1:T(8,128)S(1)}, f32[64,4,256]{2,0,1:T(8,128)S(1)}, u32[]{:S(2)}, u32[]{:S(2)}) collective-permute-start(f32[64,4,256]{2,0,1:T(8,128)S(1)} %slice.692), channel_id=1, source_target_pairs={{0,16},{4,20},{8,24},{12,28},{16,32},{20,36},{24,40},{28,44},{32,4... | collective-permute-start | bytes 786440 | tf_op jit(solution)/shard_map/ppermute | solution.py:12
  152.7 1.3 collective-permute-start.6
  154.0 5.3 %collective-permute-done.5 = f32[64,4,256]{2,0,1:T(8,128)S(1)} collective-permute-done((f32[64,4,256]{2,0,1:T(8,128)S(1)}, f32[64,4,256]{2,0,1:T(8,128)S(1)}, u32[]{:S(2)}, u32[]{:S(2)}) %collective-permute-start.5) | collective-permute-done | bytes 262176 | tf_op jit(solution)/shard_map/ppermute | solution.py:12
  159.3 5.3 %collective-permute-done.6 = f32[64,4,256]{2,0,1:T(8,128)} collective-permute-done((f32[64,4,256]{2,0,1:T(8,128)S(1)}, f32[64,4,256]{2,0,1:T(8,128)}, u32[]{:S(2)}, u32[]{:S(2)}) %collective-permute-start.6) | collective-permute-done | bytes 262176 | tf_op jit(solution)/shard_map/ppermute | solution.py:12
  165.7 12.3 %all_gather.49 = f32[256,256]{1,0:T(8,128)S(1)} all-gather(f32[64,256]{1,0:T(8,128)S(1)} %fusion.88), channel_id=1, replica_groups=mesh['leaf'=128,'sep'=4] {'sep'}, dimensions={0}, use_global_device_ids=true | all-gather | bytes 327680 | tf_op jit(solution)/shard_map/all_gather | solution.py:34
  178.9 3.6 collective-permute-start.7
  182.6 1.3 collective-permute-start.8
  183.9 3.3 collective-permute-done.7
  187.2 12.7 %collective-permute-done.8 = f32[64,3,256]{2,0,1:T(8,128)S(1)} collective-permute-done((f32[64,3,256]{2,0,1:T(8,128)S(1)}, f32[64,3,256]{2,0,1:T(8,128)S(1)}, u32[]{:S(2)}, u32[]{:S(2)}) %collective-permute-start.8) | collective-permute-done | bytes 196640 | tf_op jit(solution)/shard_map/ppermute | solution.py:12
  199.9 12.3 %all_gather.50 = f32[256,256]{1,0:T(8,128)S(1)} all-gather(f32[64,256]{1,0:T(8,128)S(1)} %fusion.86), channel_id=1, replica_groups=mesh['leaf'=128,'sep'=4] {'sep'}, dimensions={0}, use_global_device_ids=true | all-gather | bytes 327680 | tf_op jit(solution)/shard_map/all_gather | solution.py:34
  213.2 4.5 collective-permute-start.9
  217.7 1.3 collective-permute-start.10
  220.2 4.7 collective-permute-done.10
  225.8 12.3 %all_gather.51 = f32[256,256]{1,0:T(8,128)S(1)} all-gather(f32[64,256]{1,0:T(8,128)S(1)} %fusion.85), channel_id=1, replica_groups=mesh['leaf'=128,'sep'=4] {'sep'}, dimensions={0}, use_global_device_ids=true | all-gather | bytes 327680 | tf_op jit(solution)/shard_map/all_gather | solution.py:34
  239.0 3.7 collective-permute-start.11
  242.7 1.3 collective-permute-start.12
  244.6 5.2 collective-permute-done.12
  249.8 12.4 %all_gather.52 = f32[256,256]{1,0:T(8,128)S(1)} all-gather(f32[64,256]{1,0:T(8,128)S(1)} %bitcast_subtract_fusion), channel_id=1, replica_groups=mesh['leaf'=128,'sep'=4] {'sep'}, dimensions={0}, use_global_device_ids=true | all-gather | bytes 327680 | tf_op jit(solution)/shard_map/all_gather | solution.py:34
  263.5 4.7 collective-permute-start.13
  270.1 5.2 collective-permute-done.14
  275.3 12.7 %all-gather.1 = f32[256,1,256]{2,1,0:T(1,128)S(1)} all-gather(f32[64,1,256]{2,1,0:T(1,128)S(1)} %copy.70), channel_id=3, replica_groups=mesh['leaf'=128,'sep'=4] {'sep'}, dimensions={0}, use_global_device_ids=true | all-gather | bytes 327680 | tf_op jit(solution)/shard_map/all_gather | solution.py:34
  289.3 3.8 collective-permute-start.15
  295.6 4.4 collective-permute-done.16
  300.1 12.3 %all-gather.2 = f32[256,1,256]{2,1,0:T(1,128)S(1)} all-gather(f32[64,1,256]{2,1,0:T(1,128)S(1)} %copy.71), channel_id=4, replica_groups=mesh['leaf'=128,'sep'=4] {'sep'}, dimensions={0}, use_global_device_ids=true | all-gather | bytes 327680 | tf_op jit(solution)/shard_map/all_gather | solution.py:34
  313.6 6.9 %collective-permute-start.17 = (f32[64,3,256]{2,0,1:T(8,128)S(1)}, f32[64,3,256]{2,0,1:T(8,128)S(1)}, u32[]{:S(2)}, u32[]{:S(2)}) collective-permute-start(f32[64,3,256]{2,0,1:T(8,128)S(1)} %slice.705), channel_id=1, source_target_pairs={{0,32},{4,36},{8,40},{12,44},{16,48},{20,52},{24,56},{28,60},{32,6... | collective-permute-start | bytes 589832 | tf_op jit(solution)/shard_map/ppermute | solution.py:12
  321.9 2.9 collective-permute-done.17
  324.8 12.8 %collective-permute-done.18 = f32[64,3,256]{2,0,1:T(8,128)S(1)} collective-permute-done((f32[64,3,256]{2,0,1:T(8,128)S(1)}, f32[64,3,256]{2,0,1:T(8,128)S(1)}, u32[]{:S(2)}, u32[]{:S(2)}) %collective-permute-start.18) | collective-permute-done | bytes 196640 | tf_op jit(solution)/shard_map/ppermute | solution.py:12
  337.7 12.8 %all-gather.3 = f32[256,1,256]{2,1,0:T(1,128)S(1)} all-gather(f32[64,1,256]{2,1,0:T(1,128)S(1)} %copy.72), channel_id=5, replica_groups=mesh['leaf'=128,'sep'=4] {'sep'}, dimensions={0}, use_global_device_ids=true | all-gather | bytes 327680 | tf_op jit(solution)/shard_map/all_gather | solution.py:34
  352.4 1.3 collective-permute-start.19
  355.1 2.6 collective-permute-done.19
  357.7 10.0 %collective-permute-done.20 = f32[64,4,256]{2,0,1:T(8,128)S(1)} collective-permute-done((f32[64,4,256]{2,0,1:T(8,128)S(1)}, f32[64,4,256]{2,0,1:T(8,128)S(1)}, u32[]{:S(2)}, u32[]{:S(2)}) %collective-permute-start.20) | collective-permute-done | bytes 262176 | tf_op jit(solution)/shard_map/ppermute | solution.py:12
  367.9 12.3 %all-gather.4 = f32[256,1,256]{2,1,0:T(1,128)S(1)} all-gather(f32[64,1,256]{2,1,0:T(1,128)S(1)} %copy.73), channel_id=6, replica_groups=mesh['leaf'=128,'sep'=4] {'sep'}, dimensions={0}, use_global_device_ids=true | all-gather | bytes 327680 | tf_op jit(solution)/shard_map/all_gather | solution.py:34
  382.1 3.9 collective-permute-start.21
  386.0 2.0 collective-permute-start.22
  388.0 3.1 collective-permute-done.21
  391.1 5.2 %collective-permute-done.22 = f32[64,5,256]{2,0,1:T(8,128)S(1)} collective-permute-done((f32[64,5,256]{2,0,1:T(8,128)S(1)}, f32[64,5,256]{2,0,1:T(8,128)S(1)}, u32[]{:S(2)}, u32[]{:S(2)}) %collective-permute-start.22) | collective-permute-done | bytes 327712 | tf_op jit(solution)/shard_map/ppermute | solution.py:12
  396.6 12.3 %all-gather.5 = f32[256,1,256]{2,1,0:T(1,128)S(1)} all-gather(f32[64,1,256]{2,1,0:T(1,128)S(1)} %copy.74), channel_id=7, replica_groups=mesh['leaf'=128,'sep'=4] {'sep'}, dimensions={0}, use_global_device_ids=true | all-gather | bytes 327680 | tf_op jit(solution)/shard_map/all_gather | solution.py:34
  410.7 1.9 collective-permute-start.23
  412.6 3.6 collective-permute-start.24
  416.3 3.5 collective-permute-done.23
  419.8 1.8 collective-permute-done.24
  421.8 12.3 %all-gather.6 = f32[256,1,256]{2,1,0:T(1,128)S(1)} all-gather(f32[64,1,256]{2,1,0:T(1,128)S(1)} %copy.75), channel_id=8, replica_groups=mesh['leaf'=128,'sep'=4] {'sep'}, dimensions={0}, use_global_device_ids=true | all-gather | bytes 327680 | tf_op jit(solution)/shard_map/all_gather | solution.py:34
  435.4 1.9 collective-permute-start.25
  437.3 6.0 %collective-permute-done.25 = f32[64,7,256]{2,0,1:T(8,128)S(1)} collective-permute-done((f32[64,7,256]{2,0,1:T(8,128)S(1)}, f32[64,7,256]{2,0,1:T(8,128)S(1)}, u32[]{:S(2)}, u32[]{:S(2)}) %collective-permute-start.25) | collective-permute-done | bytes 458784 | tf_op jit(solution)/shard_map/ppermute | solution.py:12
  444.5 32.9 %all-gather.9.cloned.1.call-done = f32[256,7,256]{2,0,1:T(8,128)} async-done(((f32[64,7,256]{2,0,1:T(8,128)}), f32[256,7,256]{2,0,1:T(8,128)}) %all-gather.9.cloned.1.call-update) | async-done | bytes 1835024 | tf_op jit(solution)/shard_map/all_gather | solution.py:34
  477.4 2.4 convolution_select_fusion
  484.2 25.8 %reduce-scatter.7.cloned.1.call-done = f32[160,256]{1,0:T(8,128)} async-done(((f32[640,256]{1,0:T(8,128)}), f32[160,256]{1,0:T(8,128)}) %reduce-scatter.7.cloned.1.call-update) | async-done | bytes 163856
  (139 shorter events, 41.4 us)
Async XLA Ops:
  7.2 16.1 %copy-start = (f32[1,896,160]{1,2,0:T(8,128)S(1)}, f32[1,896,160]{1,2,0:T(8,128)}, u32[]{:S(2)}) copy-start(f32[1,896,160]{1,2,0:T(8,128)} %param.64) | copy-start | bytes 1720324
  7.2 60.4 %reduce-scatter.5.cloned.1.call-start = ((), (), s32[]{:S(2)}) async-start(), calls=%async_computation.2 | async-start | bytes 2621440 | tf_op jit(solution)/shard_map/reduce_scatter | solution.py:73
  23.3 1.4 copy-start.10
  24.7 3.1 copy-start.8
  27.8 52.0 %copy-start.3 = (f32[1,64,256]{2,1,0:T(8,128)S(1)}, f32[1,64,256]{2,1,0:T(8,128)}, u32[]{:S(2)}) copy-start(f32[1,64,256]{2,1,0:T(8,128)} %param.67) | copy-start | bytes 196612
  27.8 64.4 %copy-start.1 = (f32[1,256,256]{2,1,0:T(8,128)S(1)}, f32[1,256,256]{2,1,0:T(8,128)}, u32[]{:S(2)}) copy-start(f32[1,256,256]{2,1,0:T(8,128)} %param.68) | copy-start | bytes 786436
  27.8 65.0 %copy-start.2 = (f32[1,256,256]{2,1,0:T(8,128)S(1)}, f32[1,256,256]{2,1,0:T(8,128)}, u32[]{:S(2)}) copy-start(f32[1,256,256]{2,1,0:T(8,128)} %param.69) | copy-start | bytes 786436
  27.8 449.6 %all-gather.9.cloned.1.call-start = ((), (), s32[]{:S(2)}) async-start(), calls=%async_computation.3 | async-start | bytes 2293760 | tf_op jit(solution)/shard_map/all_gather | solution.py:34
  68.8 9.8 %collective-permute-start = (f32[64,7,256]{2,0,1:T(8,128)S(1)}, f32[64,7,256]{2,0,1:T(8,128)S(1)}, u32[]{:S(2)}, u32[]{:S(2)}) collective-permute-start(f32[64,7,256]{2,0,1:T(8,128)S(1)} %copy.67), channel_id=1, source_target_pairs={{0,4},{4,8},{8,12},{12,16},{16,20},{20,24},{24,28},{28,32},{32,36}... | collective-permute-start | bytes 1376264 | tf_op jit(solution)/shard_map/ppermute | solution.py:12
  93.2 9.1 %collective-permute-start.1 = (f32[64,6,256]{2,0,1:T(8,128)S(1)}, f32[64,6,256]{2,0,1:T(8,128)S(1)}, u32[]{:S(2)}, u32[]{:S(2)}) collective-permute-start(f32[64,6,256]{2,0,1:T(8,128)S(1)} %slice.686), channel_id=1, source_target_pairs={{0,4},{4,8},{8,12},{12,16},{16,20},{20,24},{24,28},{28,32},{32,36}... | collective-permute-start | bytes 1179656 | tf_op jit(solution)/shard_map/ppermute | solution.py:12
  95.2 8.9 %collective-permute-start.2 = (f32[64,6,256]{2,0,1:T(8,128)S(1)}, f32[64,6,256]{2,0,1:T(8,128)S(1)}, u32[]{:S(2)}, u32[]{:S(2)}) collective-permute-start(f32[64,6,256]{2,0,1:T(8,128)S(1)} %slice.686), channel_id=1, source_target_pairs={{4,0},{8,4},{12,8},{16,12},{20,16},{24,20},{28,24},{32,28},{36,32}... | collective-permute-start | bytes 1179656 | tf_op jit(solution)/shard_map/ppermute | solution.py:12
  117.8 10.7 %collective-permute-start.3 = (f32[64,5,256]{2,0,1:T(8,128)S(1)}, f32[64,5,256]{2,0,1:T(8,128)S(1)}, u32[]{:S(2)}, u32[]{:S(2)}) collective-permute-start(f32[64,5,256]{2,0,1:T(8,128)S(1)} %slice.689), channel_id=1, source_target_pairs={{0,8},{4,12},{8,16},{12,20},{16,24},{20,28},{24,32},{28,36},{32,40... | collective-permute-start | bytes 983048 | tf_op jit(solution)/shard_map/ppermute | solution.py:12
  121.2 11.9 %collective-permute-start.4 = (f32[64,5,256]{2,0,1:T(8,128)S(1)}, f32[64,5,256]{2,0,1:T(8,128)S(1)}, u32[]{:S(2)}, u32[]{:S(2)}) collective-permute-start(f32[64,5,256]{2,0,1:T(8,128)S(1)} %slice.689), channel_id=1, source_target_pairs={{8,0},{12,4},{16,8},{20,12},{24,16},{28,20},{32,24},{36,28},{40,32... | collective-permute-start | bytes 983048 | tf_op jit(solution)/shard_map/ppermute | solution.py:12
  146.5 12.8 %collective-permute-start.5 = (f32[64,4,256]{2,0,1:T(8,128)S(1)}, f32[64,4,256]{2,0,1:T(8,128)S(1)}, u32[]{:S(2)}, u32[]{:S(2)}) collective-permute-start(f32[64,4,256]{2,0,1:T(8,128)S(1)} %slice.692), channel_id=1, source_target_pairs={{0,16},{4,20},{8,24},{12,28},{16,32},{20,36},{24,40},{28,44},{32,4... | collective-permute-start | bytes 786440 | tf_op jit(solution)/shard_map/ppermute | solution.py:12
  152.7 12.0 %collective-permute-start.6 = (f32[64,4,256]{2,0,1:T(8,128)S(1)}, f32[64,4,256]{2,0,1:T(8,128)}, u32[]{:S(2)}, u32[]{:S(2)}) collective-permute-start(f32[64,4,256]{2,0,1:T(8,128)S(1)} %slice.692), channel_id=1, source_target_pairs={{16,0},{20,4},{24,8},{28,12},{32,16},{36,20},{40,24},{44,28},{48,3... | collective-permute-start | bytes 786440 | tf_op jit(solution)/shard_map/ppermute | solution.py:12
  178.9 8.2 %collective-permute-start.7 = (f32[64,3,256]{2,0,1:T(8,128)S(1)}, f32[64,3,256]{2,0,1:T(8,128)S(1)}, u32[]{:S(2)}, u32[]{:S(2)}) collective-permute-start(f32[64,3,256]{2,0,1:T(8,128)S(1)} %slice.695), channel_id=1, source_target_pairs={{0,32},{4,36},{8,40},{12,44},{16,48},{20,52},{24,56},{28,60},{32,6... | collective-permute-start | bytes 589832 | tf_op jit(solution)/shard_map/ppermute | solution.py:12
  182.6 17.3 %collective-permute-start.8 = (f32[64,3,256]{2,0,1:T(8,128)S(1)}, f32[64,3,256]{2,0,1:T(8,128)S(1)}, u32[]{:S(2)}, u32[]{:S(2)}) collective-permute-start(f32[64,3,256]{2,0,1:T(8,128)S(1)} %slice.695), channel_id=1, source_target_pairs={{32,0},{36,4},{40,8},{44,12},{48,16},{52,20},{56,24},{60,28},{64,3... | collective-permute-start | bytes 589832 | tf_op jit(solution)/shard_map/ppermute | solution.py:12
  213.2 7.0 %collective-permute-start.9 = (f32[64,2,256]{2,0,1:T(8,128)S(1)}, f32[64,2,256]{2,0,1:T(8,128)S(1)}, u32[]{:S(2)}, u32[]{:S(2)}) collective-permute-start(f32[64,2,256]{2,0,1:T(8,128)S(1)} %slice.698), channel_id=1, source_target_pairs={{0,64},{4,68},{8,72},{12,76},{16,80},{20,84},{24,88},{28,92},{32,9... | collective-permute-start | bytes 393224 | tf_op jit(solution)/shard_map/ppermute | solution.py:12
  217.7 7.2 %collective-permute-start.10 = (f32[64,2,256]{2,0,1:T(8,128)S(1)}, f32[64,2,256]{2,0,1:T(8,128)}, u32[]{:S(2)}, u32[]{:S(2)}) collective-permute-start(f32[64,2,256]{2,0,1:T(8,128)S(1)} %slice.698), channel_id=1, source_target_pairs={{64,0},{68,4},{72,8},{76,12},{80,16},{84,20},{88,24},{92,28},{96,3... | collective-permute-start | bytes 393224 | tf_op jit(solution)/shard_map/ppermute | solution.py:12
  239.0 5.6 %collective-permute-start.11 = (f32[64,1,256]{2,0,1:T(8,128)S(1)}, f32[64,1,256]{2,0,1:T(8,128)S(1)}, u32[]{:S(2)}, u32[]{:S(2)}) collective-permute-start(f32[64,1,256]{2,0,1:T(8,128)S(1)} %slice_add_fusion), channel_id=1, source_target_pairs={{0,128},{4,132},{8,136},{12,140},{16,144},{20,148},{24,152},{28,15... | collective-permute-start | bytes 196616 | tf_op jit(solution)/shard_map/ppermute | solution.py:12
  242.7 7.1 %collective-permute-start.12 = (f32[64,1,256]{2,0,1:T(8,128)S(1)}, f32[64,1,256]{2,0,1:T(8,128)S(1)}, u32[]{:S(2)}, u32[]{:S(2)}) collective-permute-start(f32[64,1,256]{2,0,1:T(8,128)S(1)} %slice_add_fusion), channel_id=1, source_target_pairs={{128,0},{132,4},{136,8},{140,12},{144,16},{148,20},{152,24},{156,2... | collective-permute-start | bytes 196616 | tf_op jit(solution)/shard_map/ppermute | solution.py:12
  263.5 6.6 %collective-permute-start.13 = (f32[64,1,256]{2,0,1:T(8,128)S(1)}, f32[64,1,256]{2,0,1:T(8,128)S(1)}, u32[]{:S(2)}, u32[]{:S(2)}) collective-permute-start(f32[64,1,256]{2,0,1:T(8,128)S(1)} %select_bitcast_fusion), channel_id=1, source_target_pairs={{0,128},{4,132},{8,136},{12,140},{16,144},{20,148},{24,152},{28,15... | collective-permute-start | bytes 196616 | tf_op jit(solution)/shard_map/ppermute | solution.py:12
  268.2 7.1 %collective-permute-start.14 = (f32[64,1,256]{2,0,1:T(8,128)S(1)}, f32[64,1,256]{2,0,1:T(8,128)S(1)}, u32[]{:S(2)}, u32[]{:S(2)}) collective-permute-start(f32[64,1,256]{2,0,1:T(8,128)S(1)} %select_bitcast_fusion), channel_id=1, source_target_pairs={{128,0},{132,4},{136,8},{140,12},{144,16},{148,20},{152,24},{156,2... | collective-permute-start | bytes 196616 | tf_op jit(solution)/shard_map/ppermute | solution.py:12
  289.3 6.3 %collective-permute-start.15 = (f32[64,2,256]{2,0,1:T(8,128)S(1)}, f32[64,2,256]{2,0,1:T(8,128)S(1)}, u32[]{:S(2)}, u32[]{:S(2)}) collective-permute-start(f32[64,2,256]{2,0,1:T(8,128)S(1)} %slice.702), channel_id=1, source_target_pairs={{0,64},{4,68},{8,72},{12,76},{16,80},{20,84},{24,88},{28,92},{32,9... | collective-permute-start | bytes 393224 | tf_op jit(solution)/shard_map/ppermute | solution.py:12
  293.1 6.9 %collective-permute-start.16 = (f32[64,2,256]{2,0,1:T(8,128)S(1)}, f32[64,2,256]{2,0,1:T(8,128)S(1)}, u32[]{:S(2)}, u32[]{:S(2)}) collective-permute-start(f32[64,2,256]{2,0,1:T(8,128)S(1)} %slice.702), channel_id=1, source_target_pairs={{64,0},{68,4},{72,8},{76,12},{80,16},{84,20},{88,24},{92,28},{96,3... | collective-permute-start | bytes 393224 | tf_op jit(solution)/shard_map/ppermute | solution.py:12
  313.6 11.1 %collective-permute-start.17 = (f32[64,3,256]{2,0,1:T(8,128)S(1)}, f32[64,3,256]{2,0,1:T(8,128)S(1)}, u32[]{:S(2)}, u32[]{:S(2)}) collective-permute-start(f32[64,3,256]{2,0,1:T(8,128)S(1)} %slice.705), channel_id=1, source_target_pairs={{0,32},{4,36},{8,40},{12,44},{16,48},{20,52},{24,56},{28,60},{32,6... | collective-permute-start | bytes 589832 | tf_op jit(solution)/shard_map/ppermute | solution.py:12
  320.6 17.0 %collective-permute-start.18 = (f32[64,3,256]{2,0,1:T(8,128)S(1)}, f32[64,3,256]{2,0,1:T(8,128)S(1)}, u32[]{:S(2)}, u32[]{:S(2)}) collective-permute-start(f32[64,3,256]{2,0,1:T(8,128)S(1)} %slice.705), channel_id=1, source_target_pairs={{32,0},{36,4},{40,8},{44,12},{48,16},{52,20},{56,24},{60,28},{64,3... | collective-permute-start | bytes 589832 | tf_op jit(solution)/shard_map/ppermute | solution.py:12
  352.4 5.2 %collective-permute-start.19 = (f32[64,4,256]{2,0,1:T(8,128)S(1)}, f32[64,4,256]{2,0,1:T(8,128)S(1)}, u32[]{:S(2)}, u32[]{:S(2)}) collective-permute-start(f32[64,4,256]{2,0,1:T(8,128)S(1)} %slice.708), channel_id=1, source_target_pairs={{0,16},{4,20},{8,24},{12,28},{16,32},{20,36},{24,40},{28,44},{32,4... | collective-permute-start | bytes 786440 | tf_op jit(solution)/shard_map/ppermute | solution.py:12
  353.8 13.9 %collective-permute-start.20 = (f32[64,4,256]{2,0,1:T(8,128)S(1)}, f32[64,4,256]{2,0,1:T(8,128)S(1)}, u32[]{:S(2)}, u32[]{:S(2)}) collective-permute-start(f32[64,4,256]{2,0,1:T(8,128)S(1)} %slice.708), channel_id=1, source_target_pairs={{16,0},{20,4},{24,8},{28,12},{32,16},{36,20},{40,24},{44,28},{48,3... | collective-permute-start | bytes 786440 | tf_op jit(solution)/shard_map/ppermute | solution.py:12
  382.1 9.0 %collective-permute-start.21 = (f32[64,5,256]{2,0,1:T(8,128)S(1)}, f32[64,5,256]{2,0,1:T(8,128)S(1)}, u32[]{:S(2)}, u32[]{:S(2)}) collective-permute-start(f32[64,5,256]{2,0,1:T(8,128)S(1)} %slice.711), channel_id=1, source_target_pairs={{0,8},{4,12},{8,16},{12,20},{16,24},{20,28},{24,32},{28,36},{32,40... | collective-permute-start | bytes 983048 | tf_op jit(solution)/shard_map/ppermute | solution.py:12
  386.0 10.3 %collective-permute-start.22 = (f32[64,5,256]{2,0,1:T(8,128)S(1)}, f32[64,5,256]{2,0,1:T(8,128)S(1)}, u32[]{:S(2)}, u32[]{:S(2)}) collective-permute-start(f32[64,5,256]{2,0,1:T(8,128)S(1)} %slice.711), channel_id=1, source_target_pairs={{8,0},{12,4},{16,8},{20,12},{24,16},{28,20},{32,24},{36,28},{40,32... | collective-permute-start | bytes 983048 | tf_op jit(solution)/shard_map/ppermute | solution.py:12
  410.7 9.1 %collective-permute-start.23 = (f32[64,6,256]{2,0,1:T(8,128)S(1)}, f32[64,6,256]{2,0,1:T(8,128)S(1)}, u32[]{:S(2)}, u32[]{:S(2)}) collective-permute-start(f32[64,6,256]{2,0,1:T(8,128)S(1)} %slice.714), channel_id=1, source_target_pairs={{0,4},{4,8},{8,12},{12,16},{16,20},{20,24},{24,28},{28,32},{32,36}... | collective-permute-start | bytes 1179656 | tf_op jit(solution)/shard_map/ppermute | solution.py:12
  412.6 8.9 %collective-permute-start.24 = (f32[64,6,256]{2,0,1:T(8,128)S(1)}, f32[64,6,256]{2,0,1:T(8,128)S(1)}, u32[]{:S(2)}, u32[]{:S(2)}) collective-permute-start(f32[64,6,256]{2,0,1:T(8,128)S(1)} %slice.714), channel_id=1, source_target_pairs={{4,0},{8,4},{12,8},{16,12},{20,16},{24,20},{28,24},{32,28},{36,32}... | collective-permute-start | bytes 1179656 | tf_op jit(solution)/shard_map/ppermute | solution.py:12
  434.1 10.3 %copy-start.11 = (s32[1,7]{1,0:T(1,128)S(1)}, s32[1,7]{1,0:T(1,128)}, u32[]{:S(2)}) copy-start(s32[1,7]{1,0:T(1,128)} %param.66) | copy-start | bytes 88
  434.1 43.2 %copy-start.9 = (s32[896]{0:T(1024)S(1)}, s32[896]{0:T(1024)}, u32[]{:S(2)}) copy-start(s32[896]{0:T(1024)} %copy-done.8) | copy-start | bytes 10756
  435.4 7.9 %collective-permute-start.25 = (f32[64,7,256]{2,0,1:T(8,128)S(1)}, f32[64,7,256]{2,0,1:T(8,128)S(1)}, u32[]{:S(2)}, u32[]{:S(2)}) collective-permute-start(f32[64,7,256]{2,0,1:T(8,128)S(1)} %get-tuple-element.328), channel_id=1, source_target_pairs={{4,0},{8,4},{12,8},{16,12},{20,16},{24,20},{28,24},{32,28},{36,32}... | collective-permute-start | bytes 1376264 | tf_op jit(solution)/shard_map/ppermute | solution.py:12
  444.2 65.8 %reduce-scatter.7.cloned.1.call-start = ((), (), s32[]{:S(2)}) async-start(), calls=%async_computation.4 | async-start | bytes 819200
  444.5 36.0 %copy-start.4 = (f32[1,160,640]{2,1,0:T(8,128)S(1)}, f32[1,160,640]{2,1,0:T(8,128)}, u32[]{:S(2)}) copy-start(f32[1,160,640]{2,1,0:T(8,128)} %param.63) | copy-start | bytes 1228804
  481.4 1.5 copy-start.5
  481.4 1.6 copy-start.6
  481.4 1.7 copy-start.7
Sparse Core Ops, SparseCore 0:
  27.9 39.6 reduce-scatter.4
  444.3 33.0 all-gather.8
  482.7 27.2 reduce-scatter.6
where the time goes:
time: 519 us; the launch traced here: 518 us
  waiting for transfers between devices  218 us (42%)
  blocking collectives  175 us (34%)
  starting transfers between devices  72.1 us (14%)
  matrix products  21.9 us (4%)
  between operations  15 us (3%)
  local copies, waits for them, and re-layouts  8.57 us (2%)
  other arithmetic  7.86 us (2%)
    all_gather x13, blocking collectives, sep_rows(): return lax.all_gather(payload, 'sep', axis=0, tiled=True)  161 us
    ppermute x26, waiting for transfers between devices, passed_along(): return lax.ppermute(x, axis, pairs)  120 us
    ppermute x26, starting transfers between devices, passed_along(): return lax.ppermute(x, axis, pairs)  71.8 us
    reduce_scatter x1, waiting for transfers between devices, per_device(): lax.psum_scatter(densified, 'sep', scatter_dimension=0, tiled=True)  39.7 us
    all_gather x1, waiting for transfers between devices, sep_rows(): return lax.all_gather(payload, 'sep', axis=0, tiled=True)  32.9 us
    unnamed x4, waiting for transfers between devices  25.8 us
    all_gather x1, blocking collectives, per_device(): lax.all_gather(source, 'sep', axis=0, tiled=True)  13.7 us
  transfers between devices with their start and end apart: 29, of which 29 were waited for; matrix products, arithmetic and copies ran while one was open for 0% of the time, Pallas kernels for 0%

commit v1 on v0

--- a/solution.py
+++ b/solution.py
@@ -4,6 +4,12 @@
 from jax.sharding import PartitionSpec as P
 
 highest = lax.Precision.HIGHEST
+
+
+def gather_by_exchange(x, axis, dim):
+    length = lax.axis_size(axis)
+    repeats = [length if d == dim else 1 for d in range(x.ndim)]
+    return lax.all_to_all(jnp.tile(x, repeats), axis, split_axis=dim, concat_axis=dim, tiled=True)
 
 
 def passed_along(x, axis, by):
@@ -31,7 +37,7 @@
 
 
 def sep_rows(payload):
-    return lax.all_gather(payload, "sep", axis=0, tiled=True)
+    return gather_by_exchange(payload, "sep", 0)
 
 
 def per_device(

time: 519 us -> 493 us (0.950)
  blocking collectives: 175 us -> 86.3 us
  starting transfers between devices: 72.1 us -> 108 us
  waiting for transfers between devices: 218 us -> 234 us
  local copies, waits for them, and re-layouts: 8.57 us -> 13.8 us
    all_gather x13 -> x0, blocking collectives: 161 us -> none  [sep_rows(): return lax.all_gather(payload, 'sep', axis=0, tiled=True)]
    all_to_all x0 -> x8, blocking collectives: none -> 72.6 us  [gather_by_exchange(): lax.all_to_all(jnp.tile(x, repeats), axis, split_axis=dim, concat_axis=di...]
    all_to_all x0 -> x6, waiting for transfers between devices: none -> 60 us  [gather_by_exchange(): lax.all_to_all(jnp.tile(x, repeats), axis, split_axis=dim, concat_axis=di...]
    all_gather x1 -> x0, waiting for transfers between devices: 32.9 us -> none  [sep_rows(): return lax.all_gather(payload, 'sep', axis=0, tiled=True)]
    all_to_all x0 -> x6, starting transfers between devices: none -> 22.1 us  [gather_by_exchange(): lax.all_to_all(jnp.tile(x, repeats), axis, split_axis=dim, concat_axis=di...]
    ppermute x26, starting transfers between devices: 71.8 us -> 85.9 us  [passed_along(): return lax.ppermute(x, axis, pairs)]
    ppermute x26, waiting for transfers between devices: 120 us -> 113 us  [passed_along(): return lax.ppermute(x, axis, pairs)]
    another operation x0 -> x19, local copies, waits for them, and re-layouts: none -> 5.38 us  [gather_by_exchange(): jnp.tile(x, repeats)]
  transfers between devices with their start and end apart: 29 -> 34, of which waited for: 29 -> 34; matrix products, arithmetic and copies ran while one was open for 0% -> 0% of each run, Pallas kernels for 0% -> 0%
where the time goes in v1:
time: 493 us; the launch traced here: 491 us
  waiting for transfers between devices  234 us (47%)
  starting transfers between devices  108 us (22%)
  blocking collectives  86.3 us (18%)
  matrix products  22.7 us (5%)
  between operations  15.3 us (3%)
  local copies, waits for them, and re-layouts  13.8 us (3%)
  other arithmetic  11 us (2%)
    ppermute x26, waiting for transfers between devices, passed_along(): return lax.ppermute(x, axis, pairs)  113 us
    ppermute x26, starting transfers between devices, passed_along(): return lax.ppermute(x, axis, pairs)  85.9 us
    all_to_all x8, blocking collectives, gather_by_exchange(): lax.all_to_all(jnp.tile(x, repeats), axis, split_axis=dim, concat_axis=di...  72.6 us
    all_to_all x6, waiting for transfers between devices, gather_by_exchange(): lax.all_to_all(jnp.tile(x, repeats), axis, split_axis=dim, concat_axis=di...  60 us
    reduce_scatter x1, waiting for transfers between devices, per_device(): lax.psum_scatter(densified, 'sep', scatter_dimension=0, tiled=True)  39.8 us
    all_to_all x6, starting transfers between devices, gather_by_exchange(): lax.all_to_all(jnp.tile(x, repeats), axis, split_axis=dim, concat_axis=di...  22.1 us
    unnamed x3, waiting for transfers between devices  21.8 us
    all_gather x1, blocking collectives, per_device(): lax.all_gather(source, 'sep', axis=0, tiled=True)  13.7 us
  transfers between devices with their start and end apart: 34, of which 34 were waited for; matrix products, arithmetic and copies ran while one was open for 0% of the time, Pallas kernels for 0%

profile of v1, /device:TPU:8, one launch (start us, length us, event | category | flops | bytes accessed | tf_op | source)
XLA Modules:
  0.0 491.4 jit_solution(8253437363581430895)
XLA Ops:
  7.2 13.7 %all-gather = f32[1,640,256]{2,1,0:T(8,128)S(1)} all-gather(f32[1,160,256]{2,1,0:T(8,128)} %param.62), channel_id=2, replica_groups=mesh['leaf'=128,'sep'=4] {'sep'}, dimensions={1}, use_global_device_ids=true | all-gather | bytes 819200 | tf_op jit(solution)/shard_map/all_gather | solution.py:65
  21.7 1.6 fusion.13
  25.8 1.9 copy.92
  27.8 39.8 %reduce-scatter.5.cloned.1.call-done = f32[64,7,256]{2,1,0:T(8,128)} async-done(((f32[256,7,256]{2,1,0:T(8,128)}), f32[64,7,256]{2,1,0:T(8,128)}) %reduce-scatter.5.cloned.1.call-update) | async-done | bytes 458768 | tf_op jit(solution)/shard_map/reduce_scatter | solution.py:79
  68.8 1.9 collective-permute-start
  70.7 7.9 %collective-permute-done = f32[64,7,256]{2,0,1:T(8,128)S(1)} collective-permute-done((f32[64,7,256]{2,0,1:T(8,128)S(1)}, f32[64,7,256]{2,0,1:T(8,128)S(1)}, u32[]{:S(2)}, u32[]{:S(2)}) %collective-permute-start) | collective-permute-done | bytes 458784 | tf_op jit(solution)/shard_map/ppermute | solution.py:18
  80.5 3.4 all-to-all-start
  84.0 6.6 %all-to-all-done = f32[4,64,256]{2,1,0:T(8,128)S(1)} async-done(((f32[4,64,256]{2,1,0:T(8,128)}), f32[4,64,256]{2,1,0:T(8,128)S(1)}, u32[]{:S(2)}, u32[]{:S(2)}) %all-to-all-start) | async-done | bytes 262176 | tf_op jit(solution)/shard_map/all_to_all | solution.py:12
  91.6 1.9 collective-permute-start.1
  93.6 3.6 collective-permute-start.2
  97.2 3.5 collective-permute-done.1
  100.7 1.8 collective-permute-done.2
  104.3 3.4 all-to-all-start.1
  107.8 7.1 %all-to-all-done.1 = f32[4,64,256]{2,1,0:T(8,128)S(1)} async-done(((f32[4,64,256]{2,1,0:T(8,128)}), f32[4,64,256]{2,1,0:T(8,128)S(1)}, u32[]{:S(2)}, u32[]{:S(2)}) %all-to-all-start.1) | async-done | bytes 262176 | tf_op jit(solution)/shard_map/all_to_all | solution.py:12
  115.9 2.9 collective-permute-start.3
  118.8 3.0 collective-permute-start.4
  121.8 6.3 %collective-permute-done.3 = f32[64,5,256]{2,0,1:T(8,128)S(1)} collective-permute-done((f32[64,5,256]{2,0,1:T(8,128)S(1)}, f32[64,5,256]{2,0,1:T(8,128)S(1)}, u32[]{:S(2)}, u32[]{:S(2)}) %collective-permute-start.3) | collective-permute-done | bytes 327712 | tf_op jit(solution)/shard_map/ppermute | solution.py:18
  131.1 3.4 all-to-all-start.2
  134.6 6.9 %all-to-all-done.2 = f32[4,64,256]{2,1,0:T(8,128)S(1)} async-done(((f32[4,64,256]{2,1,0:T(8,128)}), f32[4,64,256]{2,1,0:T(8,128)S(1)}, u32[]{:S(2)}, u32[]{:S(2)}) %all-to-all-start.2) | async-done | bytes 262176 | tf_op jit(solution)/shard_map/all_to_all | solution.py:12
  142.4 10.0 %collective-permute-start.5 = (f32[64,4,256]{2,0,1:T(8,128)S(1)}, f32[64,4,256]{2,0,1:T(8,128)}, u32[]{:S(2)}, u32[]{:S(2)}) collective-permute-start(f32[64,4,256]{2,0,1:T(8,128)S(1)} %slice.692), channel_id=1, source_target_pairs={{0,16},{4,20},{8,24},{12,28},{16,32},{20,36},{24,40},{28,44},{32,4... | collective-permute-start | bytes 786440 | tf_op jit(solution)/shard_map/ppermute | solution.py:18
  153.7 2.8 collective-permute-done.5
  156.5 6.9 %collective-permute-done.6 = f32[64,4,256]{2,0,1:T(8,128)} collective-permute-done((f32[64,4,256]{2,0,1:T(8,128)S(1)}, f32[64,4,256]{2,0,1:T(8,128)}, u32[]{:S(2)}, u32[]{:S(2)}) %collective-permute-start.6) | collective-permute-done | bytes 262176 | tf_op jit(solution)/shard_map/ppermute | solution.py:18
  165.2 4.1 all-to-all-start.3
  169.3 6.7 %all-to-all-done.3 = f32[4,64,256]{2,1,0:T(8,128)} async-done(((f32[4,64,256]{2,1,0:T(8,128)}), f32[4,64,256]{2,1,0:T(8,128)}, u32[]{:S(2)}, u32[]{:S(2)}) %all-to-all-start.3) | async-done | bytes 262176 | tf_op jit(solution)/shard_map/all_to_all | solution.py:12
  176.0 1.5 fusion.46
  177.9 6.0 %collective-permute-start.7 = (f32[64,3,256]{2,0,1:T(8,128)S(1)}, f32[64,3,256]{2,0,1:T(8,128)S(1)}, u32[]{:S(2)}, u32[]{:S(2)}) collective-permute-start(f32[64,3,256]{2,0,1:T(8,128)S(1)} %slice.695), channel_id=1, source_target_pairs={{0,32},{4,36},{8,40},{12,44},{16,48},{20,52},{24,56},{28,60},{32,6... | collective-permute-start | bytes 589832 | tf_op jit(solution)/shard_map/ppermute | solution.py:18
  185.3 1.8 collective-permute-done.7
  187.1 15.5 %collective-permute-done.8 = f32[64,3,256]{2,0,1:T(8,128)S(1)} collective-permute-done((f32[64,3,256]{2,0,1:T(8,128)S(1)}, f32[64,3,256]{2,0,1:T(8,128)S(1)}, u32[]{:S(2)}, u32[]{:S(2)}) %collective-permute-start.8) | collective-permute-done | bytes 196640 | tf_op jit(solution)/shard_map/ppermute | solution.py:18
  203.4 4.1 all-to-all-start.4
  207.5 6.7 %all-to-all-done.4 = f32[4,64,256]{2,1,0:T(8,128)} async-done(((f32[4,64,256]{2,1,0:T(8,128)}), f32[4,64,256]{2,1,0:T(8,128)}, u32[]{:S(2)}, u32[]{:S(2)}) %all-to-all-start.4) | async-done | bytes 262176 | tf_op jit(solution)/shard_map/all_to_all | solution.py:12
  214.2 1.5 fusion.44
  217.5 5.2 %collective-permute-start.9 = (f32[64,2,256]{2,0,1:T(8,128)S(1)}, f32[64,2,256]{2,0,1:T(8,128)}, u32[]{:S(2)}, u32[]{:S(2)}) collective-permute-start(f32[64,2,256]{2,0,1:T(8,128)S(1)} %slice.698), channel_id=1, source_target_pairs={{0,64},{4,68},{8,72},{12,76},{16,80},{20,84},{24,88},{28,92},{32,9... | collective-permute-start | bytes 393224 | tf_op jit(solution)/shard_map/ppermute | solution.py:18
  225.5 9.1 %all_to_all.122 = f32[4,64,256]{2,1,0:T(8,128)S(1)} all-to-all(f32[4,64,256]{2,1,0:T(8,128)S(1)} %tile.47), channel_id=1, replica_groups=mesh['leaf'=128,'sep'=4] {'sep'}, dimensions={0} | all-to-all | bytes 524288 | tf_op jit(solution)/shard_map/all_to_all | solution.py:12
  235.5 9.3 %collective-permute-start.11 = (f32[64,1,256]{2,0,1:T(8,128)S(1)}, f32[64,1,256]{2,0,1:T(8,128)S(1)}, u32[]{:S(2)}, u32[]{:S(2)}) collective-permute-start(f32[64,1,256]{2,0,1:T(8,128)S(1)} %slice_add_fusion), channel_id=1, source_target_pairs={{0,128},{4,132},{8,136},{12,140},{16,144},{20,148},{24,152},{28,15... | collective-permute-start | bytes 196616 | tf_op jit(solution)/shard_map/ppermute | solution.py:18
  246.7 8.7 %collective-permute-done.12 = f32[64,1,256]{2,0,1:T(8,128)S(1)} collective-permute-done((f32[64,1,256]{2,0,1:T(8,128)S(1)}, f32[64,1,256]{2,0,1:T(8,128)S(1)}, u32[]{:S(2)}, u32[]{:S(2)}) %collective-permute-start.12) | collective-permute-done | bytes 65568 | tf_op jit(solution)/shard_map/ppermute | solution.py:18
  255.5 9.1 %all_to_all.123 = f32[4,64,256]{2,1,0:T(8,128)S(1)} all-to-all(f32[4,64,256]{2,1,0:T(8,128)S(1)} %tile.48), channel_id=1, replica_groups=mesh['leaf'=128,'sep'=4] {'sep'}, dimensions={0} | all-to-all | bytes 524288 | tf_op jit(solution)/shard_map/all_to_all | solution.py:12
  265.8 6.0 %collective-permute-start.13 = (f32[64,1,256]{2,0,1:T(8,128)S(1)}, f32[64,1,256]{2,0,1:T(8,128)S(1)}, u32[]{:S(2)}, u32[]{:S(2)}) collective-permute-start(f32[64,1,256]{2,0,1:T(8,128)S(1)} %select_bitcast_fusion), channel_id=1, source_target_pairs={{0,128},{4,132},{8,136},{12,140},{16,144},{20,148},{24,152},{28,15... | collective-permute-start | bytes 196616 | tf_op jit(solution)/shard_map/ppermute | solution.py:18
  273.7 5.2 %collective-permute-done.14 = f32[64,1,256]{2,0,1:T(8,128)S(1)} collective-permute-done((f32[64,1,256]{2,0,1:T(8,128)S(1)}, f32[64,1,256]{2,0,1:T(8,128)S(1)}, u32[]{:S(2)}, u32[]{:S(2)}) %collective-permute-start.14) | collective-permute-done | bytes 65568 | tf_op jit(solution)/shard_map/ppermute | solution.py:18
  278.9 9.1 %all_to_all.124 = f32[4,64,256]{2,1,0:T(8,128)S(1)} all-to-all(f32[4,64,256]{2,1,0:T(8,128)S(1)} %tile.50), channel_id=1, replica_groups=mesh['leaf'=128,'sep'=4] {'sep'}, dimensions={0} | all-to-all | bytes 524288 | tf_op jit(solution)/shard_map/all_to_all | solution.py:12
  293.8 4.6 collective-permute-done.16
  298.5 9.1 %all_to_all.125 = f32[4,64,256]{2,1,0:T(8,128)S(1)} all-to-all(f32[4,64,256]{2,1,0:T(8,128)S(1)} %tile.52), channel_id=1, replica_groups=mesh['leaf'=128,'sep'=4] {'sep'}, dimensions={0} | all-to-all | bytes 524288 | tf_op jit(solution)/shard_map/all_to_all | solution.py:12
  309.4 5.1 %collective-permute-start.17 = (f32[64,3,256]{2,0,1:T(8,128)S(1)}, f32[64,3,256]{2,0,1:T(8,128)S(1)}, u32[]{:S(2)}, u32[]{:S(2)}) collective-permute-start(f32[64,3,256]{2,0,1:T(8,128)S(1)} %slice.705), channel_id=1, source_target_pairs={{0,32},{4,36},{8,40},{12,44},{16,48},{20,52},{24,56},{28,60},{32,6... | collective-permute-start | bytes 589832 | tf_op jit(solution)/shard_map/ppermute | solution.py:18
  315.8 3.2 collective-permute-done.17
  319.0 9.0 %collective-permute-done.18 = f32[64,3,256]{2,0,1:T(8,128)S(1)} collective-permute-done((f32[64,3,256]{2,0,1:T(8,128)S(1)}, f32[64,3,256]{2,0,1:T(8,128)S(1)}, u32[]{:S(2)}, u32[]{:S(2)}) %collective-permute-start.18) | collective-permute-done | bytes 196640 | tf_op jit(solution)/shard_map/ppermute | solution.py:18
  328.2 9.1 %all_to_all.126 = f32[4,64,256]{2,1,0:T(8,128)S(1)} all-to-all(f32[4,64,256]{2,1,0:T(8,128)S(1)} %tile.54), channel_id=1, replica_groups=mesh['leaf'=128,'sep'=4] {'sep'}, dimensions={0} | all-to-all | bytes 524288 | tf_op jit(solution)/shard_map/all_to_all | solution.py:12
  342.0 2.5 collective-permute-done.19
  344.5 8.3 %collective-permute-done.20 = f32[64,4,256]{2,0,1:T(8,128)S(1)} collective-permute-done((f32[64,4,256]{2,0,1:T(8,128)S(1)}, f32[64,4,256]{2,0,1:T(8,128)S(1)}, u32[]{:S(2)}, u32[]{:S(2)}) %collective-permute-start.20) | collective-permute-done | bytes 262176 | tf_op jit(solution)/shard_map/ppermute | solution.py:18
  352.9 9.1 %all_to_all.127 = f32[4,64,256]{2,1,0:T(8,128)S(1)} all-to-all(f32[4,64,256]{2,1,0:T(8,128)S(1)} %tile.56), channel_id=1, replica_groups=mesh['leaf'=128,'sep'=4] {'sep'}, dimensions={0} | all-to-all | bytes 524288 | tf_op jit(solution)/shard_map/all_to_all | solution.py:12
  363.9 7.7 %collective-permute-start.21 = (f32[64,5,256]{2,0,1:T(8,128)S(1)}, f32[64,5,256]{2,0,1:T(8,128)S(1)}, u32[]{:S(2)}, u32[]{:S(2)}) collective-permute-start(f32[64,5,256]{2,0,1:T(8,128)S(1)} %slice.711), channel_id=1, source_target_pairs={{0,8},{4,12},{8,16},{12,20},{16,24},{20,28},{24,32},{28,36},{32,40... | collective-permute-start | bytes 983048 | tf_op jit(solution)/shard_map/ppermute | solution.py:18
  371.6 1.9 collective-permute-start.22
  373.5 2.6 collective-permute-done.21
  376.1 5.5 %collective-permute-done.22 = f32[64,5,256]{2,0,1:T(8,128)S(1)} collective-permute-done((f32[64,5,256]{2,0,1:T(8,128)S(1)}, f32[64,5,256]{2,0,1:T(8,128)S(1)}, u32[]{:S(2)}, u32[]{:S(2)}) %collective-permute-start.22) | collective-permute-done | bytes 327712 | tf_op jit(solution)/shard_map/ppermute | solution.py:18
  381.9 9.1 %all_to_all.128 = f32[4,64,256]{2,1,0:T(8,128)S(1)} all-to-all(f32[4,64,256]{2,1,0:T(8,128)S(1)} %tile.58), channel_id=1, replica_groups=mesh['leaf'=128,'sep'=4] {'sep'}, dimensions={0} | all-to-all | bytes 524288 | tf_op jit(solution)/shard_map/all_to_all | solution.py:12
  392.8 1.9 collective-permute-start.23
  394.7 3.6 collective-permute-start.24
  398.4 3.5 collective-permute-done.23
  401.9 1.8 collective-permute-done.24
  403.9 9.1 %all_to_all.129 = f32[4,64,256]{2,1,0:T(8,128)S(1)} all-to-all(f32[4,64,256]{2,1,0:T(8,128)S(1)} %tile.60), channel_id=1, replica_groups=mesh['leaf'=128,'sep'=4] {'sep'}, dimensions={0} | all-to-all | bytes 524288 | tf_op jit(solution)/shard_map/all_to_all | solution.py:12
  414.9 2.6 collective-permute-start.25
  417.5 6.0 %collective-permute-done.25 = f32[64,7,256]{2,0,1:T(8,128)S(1)} collective-permute-done((f32[64,7,256]{2,0,1:T(8,128)S(1)}, f32[64,7,256]{2,0,1:T(8,128)S(1)}, u32[]{:S(2)}, u32[]{:S(2)}) %collective-permute-start.25) | collective-permute-done | bytes 458784 | tf_op jit(solution)/shard_map/ppermute | solution.py:18
  423.8 1.5 tile.61
  425.3 3.7 all-to-all-start.13
  429.2 26.0 %all-to-all-done.13 = f32[256,7,256]{2,1,0:T(8,128)S(1)} async-done(((f32[256,7,256]{2,1,0:T(8,128)}), f32[256,7,256]{2,1,0:T(8,128)S(1)}, u32[]{:S(2)}, u32[]{:S(2)}) %all-to-all-start.13) | async-done | bytes 1835040 | tf_op jit(solution)/shard_map/all_to_all | solution.py:12
  460.9 21.8 %reduce-scatter.7.cloned.1.call-done = f32[160,256]{1,0:T(8,128)} async-done(((f32[640,256]{1,0:T(8,128)}), f32[160,256]{1,0:T(8,128)}) %reduce-scatter.7.cloned.1.call-update) | async-done | bytes 163856
  (154 shorter events, 58.0 us)
Async XLA Ops:
  7.2 16.1 %copy-start = (f32[1,896,160]{1,2,0:T(8,128)S(1)}, f32[1,896,160]{1,2,0:T(8,128)}, u32[]{:S(2)}) copy-start(f32[1,896,160]{1,2,0:T(8,128)} %param.64) | copy-start | bytes 1720324
  7.2 60.4 %reduce-scatter.5.cloned.1.call-start = ((), (), s32[]{:S(2)}) async-start(), calls=%async_computation.16 | async-start | bytes 2621440 | tf_op jit(solution)/shard_map/reduce_scatter | solution.py:79
  21.7 3.0 copy-start.11
  27.7 52.0 %copy-start.3 = (f32[1,64,256]{2,1,0:T(8,128)S(1)}, f32[1,64,256]{2,1,0:T(8,128)}, u32[]{:S(2)}) copy-start(f32[1,64,256]{2,1,0:T(8,128)} %param.67) | copy-start | bytes 196612
  27.8 62.8 %copy-start.1 = (f32[1,256,256]{2,1,0:T(8,128)S(1)}, f32[1,256,256]{2,1,0:T(8,128)}, u32[]{:S(2)}) copy-start(f32[1,256,256]{2,1,0:T(8,128)} %param.68) | copy-start | bytes 786436
  27.8 63.4 %copy-start.2 = (f32[1,256,256]{2,1,0:T(8,128)S(1)}, f32[1,256,256]{2,1,0:T(8,128)}, u32[]{:S(2)}) copy-start(f32[1,256,256]{2,1,0:T(8,128)} %param.69) | copy-start | bytes 786436
  68.8 9.8 %collective-permute-start = (f32[64,7,256]{2,0,1:T(8,128)S(1)}, f32[64,7,256]{2,0,1:T(8,128)S(1)}, u32[]{:S(2)}, u32[]{:S(2)}) collective-permute-start(f32[64,7,256]{2,0,1:T(8,128)S(1)} %copy.93), channel_id=1, source_target_pairs={{0,4},{4,8},{8,12},{12,16},{16,20},{20,24},{24,28},{28,32},{32,36}... | collective-permute-start | bytes 1376264 | tf_op jit(solution)/shard_map/ppermute | solution.py:18
  80.5 10.1 %all-to-all-start = ((f32[4,64,256]{2,1,0:T(8,128)}), f32[4,64,256]{2,1,0:T(8,128)S(1)}, u32[]{:S(2)}, u32[]{:S(2)}) async-start(f32[4,64,256]{2,1,0:T(8,128)} %tile.42), calls=%async_computation.1 | async-start | bytes 524288 | tf_op jit(solution)/shard_map/all_to_all | solution.py:12
  91.6 9.1 %collective-permute-start.1 = (f32[64,6,256]{2,0,1:T(8,128)S(1)}, f32[64,6,256]{2,0,1:T(8,128)S(1)}, u32[]{:S(2)}, u32[]{:S(2)}) collective-permute-start(f32[64,6,256]{2,0,1:T(8,128)S(1)} %slice.686), channel_id=1, source_target_pairs={{0,4},{4,8},{8,12},{12,16},{16,20},{20,24},{24,28},{28,32},{32,36}... | collective-permute-start | bytes 1179656 | tf_op jit(solution)/shard_map/ppermute | solution.py:18
  93.6 8.9 %collective-permute-start.2 = (f32[64,6,256]{2,0,1:T(8,128)S(1)}, f32[64,6,256]{2,0,1:T(8,128)}, u32[]{:S(2)}, u32[]{:S(2)}) collective-permute-start(f32[64,6,256]{2,0,1:T(8,128)S(1)} %slice.686), channel_id=1, source_target_pairs={{4,0},{8,4},{12,8},{16,12},{20,16},{24,20},{28,24},{32,28},{36,32}... | collective-permute-start | bytes 1179656 | tf_op jit(solution)/shard_map/ppermute | solution.py:18
  104.3 10.6 %all-to-all-start.1 = ((f32[4,64,256]{2,1,0:T(8,128)}), f32[4,64,256]{2,1,0:T(8,128)S(1)}, u32[]{:S(2)}, u32[]{:S(2)}) async-start(f32[4,64,256]{2,1,0:T(8,128)} %tile.43), calls=%async_computation.2 | async-start | bytes 524288 | tf_op jit(solution)/shard_map/all_to_all | solution.py:12
  115.9 12.2 %collective-permute-start.3 = (f32[64,5,256]{2,0,1:T(8,128)S(1)}, f32[64,5,256]{2,0,1:T(8,128)S(1)}, u32[]{:S(2)}, u32[]{:S(2)}) collective-permute-start(f32[64,5,256]{2,0,1:T(8,128)S(1)} %slice.689), channel_id=1, source_target_pairs={{0,8},{4,12},{8,16},{12,20},{16,24},{20,28},{24,32},{28,36},{32,40... | collective-permute-start | bytes 983048 | tf_op jit(solution)/shard_map/ppermute | solution.py:18
  118.8 10.5 %collective-permute-start.4 = (f32[64,5,256]{2,0,1:T(8,128)S(1)}, f32[64,5,256]{2,0,1:T(8,128)}, u32[]{:S(2)}, u32[]{:S(2)}) collective-permute-start(f32[64,5,256]{2,0,1:T(8,128)S(1)} %slice.689), channel_id=1, source_target_pairs={{8,0},{12,4},{16,8},{20,12},{24,16},{28,20},{32,24},{36,28},{40,32... | collective-permute-start | bytes 983048 | tf_op jit(solution)/shard_map/ppermute | solution.py:18
  131.1 10.3 %all-to-all-start.2 = ((f32[4,64,256]{2,1,0:T(8,128)}), f32[4,64,256]{2,1,0:T(8,128)S(1)}, u32[]{:S(2)}, u32[]{:S(2)}) async-start(f32[4,64,256]{2,1,0:T(8,128)} %tile.44), calls=%async_computation.3 | async-start | bytes 524288 | tf_op jit(solution)/shard_map/all_to_all | solution.py:12
  142.4 14.0 %collective-permute-start.5 = (f32[64,4,256]{2,0,1:T(8,128)S(1)}, f32[64,4,256]{2,0,1:T(8,128)}, u32[]{:S(2)}, u32[]{:S(2)}) collective-permute-start(f32[64,4,256]{2,0,1:T(8,128)S(1)} %slice.692), channel_id=1, source_target_pairs={{0,16},{4,20},{8,24},{12,28},{16,32},{20,36},{24,40},{28,44},{32,4... | collective-permute-start | bytes 786440 | tf_op jit(solution)/shard_map/ppermute | solution.py:18
  152.4 11.0 %collective-permute-start.6 = (f32[64,4,256]{2,0,1:T(8,128)S(1)}, f32[64,4,256]{2,0,1:T(8,128)}, u32[]{:S(2)}, u32[]{:S(2)}) collective-permute-start(f32[64,4,256]{2,0,1:T(8,128)S(1)} %slice.692), channel_id=1, source_target_pairs={{16,0},{20,4},{24,8},{28,12},{32,16},{36,20},{40,24},{44,28},{48,3... | collective-permute-start | bytes 786440 | tf_op jit(solution)/shard_map/ppermute | solution.py:18
  165.2 10.8 %all-to-all-start.3 = ((f32[4,64,256]{2,1,0:T(8,128)}), f32[4,64,256]{2,1,0:T(8,128)}, u32[]{:S(2)}, u32[]{:S(2)}) async-start(f32[4,64,256]{2,1,0:T(8,128)} %tile.45), calls=%async_computation.4 | async-start | bytes 524288 | tf_op jit(solution)/shard_map/all_to_all | solution.py:12
  177.9 9.2 %collective-permute-start.7 = (f32[64,3,256]{2,0,1:T(8,128)S(1)}, f32[64,3,256]{2,0,1:T(8,128)S(1)}, u32[]{:S(2)}, u32[]{:S(2)}) collective-permute-start(f32[64,3,256]{2,0,1:T(8,128)S(1)} %slice.695), channel_id=1, source_target_pairs={{0,32},{4,36},{8,40},{12,44},{16,48},{20,52},{24,56},{28,60},{32,6... | collective-permute-start | bytes 589832 | tf_op jit(solution)/shard_map/ppermute | solution.py:18
  184.0 18.6 %collective-permute-start.8 = (f32[64,3,256]{2,0,1:T(8,128)S(1)}, f32[64,3,256]{2,0,1:T(8,128)S(1)}, u32[]{:S(2)}, u32[]{:S(2)}) collective-permute-start(f32[64,3,256]{2,0,1:T(8,128)S(1)} %slice.695), channel_id=1, source_target_pairs={{32,0},{36,4},{40,8},{44,12},{48,16},{52,20},{56,24},{60,28},{64,3... | collective-permute-start | bytes 589832 | tf_op jit(solution)/shard_map/ppermute | solution.py:18
  203.4 10.8 %all-to-all-start.4 = ((f32[4,64,256]{2,1,0:T(8,128)}), f32[4,64,256]{2,1,0:T(8,128)}, u32[]{:S(2)}, u32[]{:S(2)}) async-start(f32[4,64,256]{2,1,0:T(8,128)} %tile.46), calls=%async_computation.5 | async-start | bytes 524288 | tf_op jit(solution)/shard_map/all_to_all | solution.py:12
  216.2 6.9 %collective-permute-start.10 = (f32[64,2,256]{2,0,1:T(8,128)S(1)}, f32[64,2,256]{2,0,1:T(8,128)S(1)}, u32[]{:S(2)}, u32[]{:S(2)}) collective-permute-start(f32[64,2,256]{2,0,1:T(8,128)S(1)} %slice.698), channel_id=1, source_target_pairs={{64,0},{68,4},{72,8},{76,12},{80,16},{84,20},{88,24},{92,28},{96,3... | collective-permute-start | bytes 393224 | tf_op jit(solution)/shard_map/ppermute | solution.py:18
  217.5 7.1 %collective-permute-start.9 = (f32[64,2,256]{2,0,1:T(8,128)S(1)}, f32[64,2,256]{2,0,1:T(8,128)}, u32[]{:S(2)}, u32[]{:S(2)}) collective-permute-start(f32[64,2,256]{2,0,1:T(8,128)S(1)} %slice.698), channel_id=1, source_target_pairs={{0,64},{4,68},{8,72},{12,76},{16,80},{20,84},{24,88},{28,92},{32,9... | collective-permute-start | bytes 393224 | tf_op jit(solution)/shard_map/ppermute | solution.py:18
  235.5 11.2 %collective-permute-start.11 = (f32[64,1,256]{2,0,1:T(8,128)S(1)}, f32[64,1,256]{2,0,1:T(8,128)S(1)}, u32[]{:S(2)}, u32[]{:S(2)}) collective-permute-start(f32[64,1,256]{2,0,1:T(8,128)S(1)} %slice_add_fusion), channel_id=1, source_target_pairs={{0,128},{4,132},{8,136},{12,140},{16,144},{20,148},{24,152},{28,15... | collective-permute-start | bytes 196616 | tf_op jit(solution)/shard_map/ppermute | solution.py:18
  244.9 10.6 %collective-permute-start.12 = (f32[64,1,256]{2,0,1:T(8,128)S(1)}, f32[64,1,256]{2,0,1:T(8,128)S(1)}, u32[]{:S(2)}, u32[]{:S(2)}) collective-permute-start(f32[64,1,256]{2,0,1:T(8,128)S(1)} %slice_add_fusion), channel_id=1, source_target_pairs={{128,0},{132,4},{136,8},{140,12},{144,16},{148,20},{152,24},{156,2... | collective-permute-start | bytes 196616 | tf_op jit(solution)/shard_map/ppermute | solution.py:18
  265.8 7.9 %collective-permute-start.13 = (f32[64,1,256]{2,0,1:T(8,128)S(1)}, f32[64,1,256]{2,0,1:T(8,128)S(1)}, u32[]{:S(2)}, u32[]{:S(2)}) collective-permute-start(f32[64,1,256]{2,0,1:T(8,128)S(1)} %select_bitcast_fusion), channel_id=1, source_target_pairs={{0,128},{4,132},{8,136},{12,140},{16,144},{20,148},{24,152},{28,15... | collective-permute-start | bytes 196616 | tf_op jit(solution)/shard_map/ppermute | solution.py:18
  271.8 7.1 %collective-permute-start.14 = (f32[64,1,256]{2,0,1:T(8,128)S(1)}, f32[64,1,256]{2,0,1:T(8,128)S(1)}, u32[]{:S(2)}, u32[]{:S(2)}) collective-permute-start(f32[64,1,256]{2,0,1:T(8,128)S(1)} %select_bitcast_fusion), channel_id=1, source_target_pairs={{128,0},{132,4},{136,8},{140,12},{144,16},{148,20},{152,24},{156,2... | collective-permute-start | bytes 196616 | tf_op jit(solution)/shard_map/ppermute | solution.py:18
  289.8 3.9 collective-permute-start.15
  291.3 7.1 %collective-permute-start.16 = (f32[64,2,256]{2,0,1:T(8,128)S(1)}, f32[64,2,256]{2,0,1:T(8,128)S(1)}, u32[]{:S(2)}, u32[]{:S(2)}) collective-permute-start(f32[64,2,256]{2,0,1:T(8,128)S(1)} %slice.702), channel_id=1, source_target_pairs={{64,0},{68,4},{72,8},{76,12},{80,16},{84,20},{88,24},{92,28},{96,3... | collective-permute-start | bytes 393224 | tf_op jit(solution)/shard_map/ppermute | solution.py:18
  309.4 9.6 %collective-permute-start.17 = (f32[64,3,256]{2,0,1:T(8,128)S(1)}, f32[64,3,256]{2,0,1:T(8,128)S(1)}, u32[]{:S(2)}, u32[]{:S(2)}) collective-permute-start(f32[64,3,256]{2,0,1:T(8,128)S(1)} %slice.705), channel_id=1, source_target_pairs={{0,32},{4,36},{8,40},{12,44},{16,48},{20,52},{24,56},{28,60},{32,6... | collective-permute-start | bytes 589832 | tf_op jit(solution)/shard_map/ppermute | solution.py:18
  314.5 13.6 %collective-permute-start.18 = (f32[64,3,256]{2,0,1:T(8,128)S(1)}, f32[64,3,256]{2,0,1:T(8,128)S(1)}, u32[]{:S(2)}, u32[]{:S(2)}) collective-permute-start(f32[64,3,256]{2,0,1:T(8,128)S(1)} %slice.705), channel_id=1, source_target_pairs={{32,0},{36,4},{40,8},{44,12},{48,16},{52,20},{56,24},{60,28},{64,3... | collective-permute-start | bytes 589832 | tf_op jit(solution)/shard_map/ppermute | solution.py:18
  339.1 5.4 %collective-permute-start.19 = (f32[64,4,256]{2,0,1:T(8,128)S(1)}, f32[64,4,256]{2,0,1:T(8,128)S(1)}, u32[]{:S(2)}, u32[]{:S(2)}) collective-permute-start(f32[64,4,256]{2,0,1:T(8,128)S(1)} %slice.708), channel_id=1, source_target_pairs={{0,16},{4,20},{8,24},{12,28},{16,32},{20,36},{24,40},{28,44},{32,4... | collective-permute-start | bytes 786440 | tf_op jit(solution)/shard_map/ppermute | solution.py:18
  340.6 12.1 %collective-permute-start.20 = (f32[64,4,256]{2,0,1:T(8,128)S(1)}, f32[64,4,256]{2,0,1:T(8,128)S(1)}, u32[]{:S(2)}, u32[]{:S(2)}) collective-permute-start(f32[64,4,256]{2,0,1:T(8,128)S(1)} %slice.708), channel_id=1, source_target_pairs={{16,0},{20,4},{24,8},{28,12},{32,16},{36,20},{40,24},{44,28},{48,3... | collective-permute-start | bytes 786440 | tf_op jit(solution)/shard_map/ppermute | solution.py:18
  363.9 12.2 %collective-permute-start.21 = (f32[64,5,256]{2,0,1:T(8,128)S(1)}, f32[64,5,256]{2,0,1:T(8,128)S(1)}, u32[]{:S(2)}, u32[]{:S(2)}) collective-permute-start(f32[64,5,256]{2,0,1:T(8,128)S(1)} %slice.711), channel_id=1, source_target_pairs={{0,8},{4,12},{8,16},{12,20},{16,24},{20,28},{24,32},{28,36},{32,40... | collective-permute-start | bytes 983048 | tf_op jit(solution)/shard_map/ppermute | solution.py:18
  371.6 10.1 %collective-permute-start.22 = (f32[64,5,256]{2,0,1:T(8,128)S(1)}, f32[64,5,256]{2,0,1:T(8,128)S(1)}, u32[]{:S(2)}, u32[]{:S(2)}) collective-permute-start(f32[64,5,256]{2,0,1:T(8,128)S(1)} %slice.711), channel_id=1, source_target_pairs={{8,0},{12,4},{16,8},{20,12},{24,16},{28,20},{32,24},{36,28},{40,32... | collective-permute-start | bytes 983048 | tf_op jit(solution)/shard_map/ppermute | solution.py:18
  392.8 9.1 %collective-permute-start.23 = (f32[64,6,256]{2,0,1:T(8,128)S(1)}, f32[64,6,256]{2,0,1:T(8,128)S(1)}, u32[]{:S(2)}, u32[]{:S(2)}) collective-permute-start(f32[64,6,256]{2,0,1:T(8,128)S(1)} %slice.714), channel_id=1, source_target_pairs={{0,4},{4,8},{8,12},{12,16},{16,20},{20,24},{24,28},{28,32},{32,36}... | collective-permute-start | bytes 1179656 | tf_op jit(solution)/shard_map/ppermute | solution.py:18
  394.7 8.9 %collective-permute-start.24 = (f32[64,6,256]{2,0,1:T(8,128)S(1)}, f32[64,6,256]{2,0,1:T(8,128)S(1)}, u32[]{:S(2)}, u32[]{:S(2)}) collective-permute-start(f32[64,6,256]{2,0,1:T(8,128)S(1)} %slice.714), channel_id=1, source_target_pairs={{4,0},{8,4},{12,8},{16,12},{20,16},{24,20},{28,24},{32,28},{36,32}... | collective-permute-start | bytes 1179656 | tf_op jit(solution)/shard_map/ppermute | solution.py:18
  414.9 8.6 %collective-permute-start.25 = (f32[64,7,256]{2,0,1:T(8,128)S(1)}, f32[64,7,256]{2,0,1:T(8,128)S(1)}, u32[]{:S(2)}, u32[]{:S(2)}) collective-permute-start(f32[64,7,256]{2,0,1:T(8,128)S(1)} %get-tuple-element.328), channel_id=1, source_target_pairs={{4,0},{8,4},{12,8},{16,12},{20,16},{24,20},{28,24},{32,28},{36,32}... | collective-permute-start | bytes 1376264 | tf_op jit(solution)/shard_map/ppermute | solution.py:18
  425.3 3.8 copy-start.12
  425.3 29.9 %all-to-all-start.13 = ((f32[256,7,256]{2,1,0:T(8,128)}), f32[256,7,256]{2,1,0:T(8,128)S(1)}, u32[]{:S(2)}, u32[]{:S(2)}) async-start(f32[256,7,256]{2,1,0:T(8,128)} %bitcast.65), calls=%async_computation.14 | async-start | bytes 4194304 | tf_op jit(solution)/shard_map/all_to_all | solution.py:12
  429.1 53.6 %reduce-scatter.7.cloned.1.call-start = ((), (), s32[]{:S(2)}) async-start(), calls=%async_computation.17 | async-start | bytes 819200
  429.2 28.1 %copy-start.4 = (f32[1,160,640]{2,1,0:T(8,128)S(1)}, f32[1,160,640]{2,1,0:T(8,128)}, u32[]{:S(2)}) copy-start(f32[1,160,640]{2,1,0:T(8,128)} %param.63) | copy-start | bytes 1228804
  457.3 2.2 copy-start.5
  457.3 2.3 copy-start.6
  457.3 2.4 copy-start.7
  458.2 1.6 copy-start.8
  458.2 1.7 copy-start.9
  458.2 1.8 copy-start.10
Sparse Core Ops, SparseCore 0:
  27.9 39.6 reduce-scatter.4
  459.4 23.2 reduce-scatter.6
